TPU v7x, 128 devices: a whole 4x4x4 slice. The times are simulated.
128 devices in a mesh: req: 32 (over x, y, core), head: 4 (over z).
Axes of the slice: x: 4, y: 4, z: 4, core: 2. Of those that a mesh axis runs over, the one named last changes fastest.
Arguments:
- prefill_query: bfloat16 [16384, 2048], P('req', 'head'), may hold values from -16 to 16
- prefill_new_pairs: bfloat16 [16384, 2, 1024], P('req', None, 'head'), may hold values from -16 to 16
- prefill_cache: bfloat16 [32, 2, 2048, 1024], P('req', None, None, 'head'), may hold values from -16 to 16
- prefill_start: int32 [32], P('req'), may hold values from 0 to 2048, as said below
- decode_query: bfloat16 [96, 2048], P('req', 'head'), may hold values from -16 to 16
- decode_fresh: bfloat16 [96, 2, 1024], P('req', None, 'head'), may hold values from -16 to 16
- decode_cache: bfloat16 [96, 2, 2048, 1024], P('req', None, None, 'head'), may hold values from -16 to 16
- decode_length: int32 [96], P('req'), may hold values from 2 to 2048
- decode_slot: int32 [96], P('req'), may hold values from 0 to 95, each once
- prefill_states: bfloat16 [16384, 2048], P('req', 'head'), may hold values from -32 to 32
- decode_states: bfloat16 [96, 2048], P('req', 'head'), may hold values from -32 to 32
- output_proj: bfloat16 [2048, 2048], P('head', 'req'), may hold values from -0.125 to 0.125
- norm_gain: bfloat16 [2048], replicated, may hold values from 0.099609375 to 1.8984375
- gate_weight: bfloat16 [2048, 6144], P('req', 'head'), may hold values from -0.125 to 0.125
- up_weight: bfloat16 [2048, 6144], P('req', 'head'), may hold values from -0.125 to 0.125
- down_weight: bfloat16 [6144, 2048], P('head', 'req'), may hold values from -0.078125 to 0.078125
Outputs:
- prefill_result: bfloat16 [16384, 2048], P('req', 'head')
- decode_result: bfloat16 [96, 2048], P('req', 'head')
Inputs may be any that keep to these rules, and one draw needn't show every extreme that they name: `decode_slot`: a permutation; the cache of slot s is held by req index s // 3. `prefill_start`: a multiple of 512.
All inputs are finite; a program needn't handle non-finite values.
Results may differ from a plain program's by a relative error of at most 0.0094.
Values may be sent and summed in bfloat16 or wider, within the bound.
No kernel may reach another device: no remote copies, remote signals or barrier semaphores. Data moves between devices by JAX's collectives and lax.ppermute only.
A program may use at most 128 MiB of HBM per device.

v0:
```python
import math
import jax
import jax.numpy as jnp
from jax import lax
from jax.sharding import PartitionSpec as P

HEAD_SIZE = 128
REQUEST_TOKENS = 512
rope_base = 1000000.0
norm_eps = 1e-06


def rope_tables(positions, head_size):
    half_size = head_size // 2
    lane_index = jnp.arange(half_size, dtype=jnp.float32)
    inverse = jnp.power(jnp.float32(rope_base), -2.0 * lane_index / head_size)
    angles = positions.astype(jnp.float32)[:, None] * inverse[None, :]
    cosine = jnp.concatenate([jnp.cos(angles), jnp.cos(angles)], axis=1)
    sine_table = jnp.concatenate([jnp.sin(angles), jnp.sin(angles)], axis=1)
    return (cosine, sine_table)


def rotate(vectors, cosine, sine_table):
    half_size = vectors.shape[-1] // 2
    front_half = vectors[..., :half_size]
    back_half = vectors[..., half_size:]
    turned = jnp.concatenate([-back_half, front_half], axis=-1)
    return vectors * cosine[:, None, :] + turned * sine_table[:, None, :]


def attend(query_rows, key_rows, value_rows, visible):
    row_count, head_count, head_size = query_rows.shape
    groups = key_rows.shape[1]
    grouped = query_rows.reshape(row_count, groups, head_count // groups, head_size)
    scores = jnp.einsum("qhgd,khd->hgqk", grouped, key_rows, preferred_element_type=jnp.float32) * (
        1.0 / math.sqrt(head_size)
    )
    scores = jnp.where(visible[None, None], scores, -jnp.inf)
    highest = jnp.max(scores, axis=-1, keepdims=True)
    unnormed = jnp.exp(scores - highest)
    totals = jnp.sum(unnormed, axis=-1, keepdims=True)
    rounded = unnormed.astype(jnp.bfloat16)
    blended = jnp.einsum("hgqk,khd->qhgd", rounded, value_rows, preferred_element_type=jnp.float32)
    blended = blended / jnp.transpose(totals, (2, 0, 1, 3))
    return blended.reshape(row_count, head_count * head_size).astype(jnp.bfloat16)


def prefill_task(query_rows, fresh_rows, cache_rows, offset_value, head_size):
    span_len = query_rows.shape[0]
    positions = offset_value + jnp.arange(span_len, dtype=jnp.int32)
    cosine, sine_table = rope_tables(positions, head_size)
    head_count = query_rows.shape[1] // head_size
    groups = fresh_rows.shape[2] // head_size
    rot_query = rotate(
        query_rows.astype(jnp.float32).reshape(span_len, head_count, head_size), cosine, sine_table
    ).astype(jnp.bfloat16)
    rot_key = rotate(
        fresh_rows[:, 0].astype(jnp.float32).reshape(span_len, groups, head_size),
        cosine,
        sine_table,
    ).astype(jnp.bfloat16)
    cache_len = cache_rows.shape[1]
    key_rows = jnp.concatenate(
        [cache_rows[0].reshape(cache_len, groups, head_size), rot_key], axis=0
    )
    value_rows = jnp.concatenate(
        [
            cache_rows[1].reshape(cache_len, groups, head_size),
            fresh_rows[:, 1].reshape(span_len, groups, head_size),
        ],
        axis=0,
    )
    cache_seen = jnp.broadcast_to(
        jnp.arange(cache_len, dtype=jnp.int32)[None, :] < offset_value, (span_len, cache_len)
    )
    own_seen = (
        jnp.arange(span_len, dtype=jnp.int32)[None, :]
        <= jnp.arange(span_len, dtype=jnp.int32)[:, None]
    )
    visible = jnp.concatenate([cache_seen, own_seen], axis=1)
    return attend(rot_query, key_rows, value_rows, visible)


def decode_task(query_rows, fresh_rows, cache_rows, length, head_size):
    positions = jnp.reshape(length, (1,))
    cosine, sine_table = rope_tables(positions, head_size)
    head_count = query_rows.shape[0] // head_size
    groups = fresh_rows.shape[1] // head_size
    rot_query = rotate(
        query_rows.astype(jnp.float32).reshape(1, head_count, head_size), cosine, sine_table
    ).astype(jnp.bfloat16)
    rot_key = rotate(
        fresh_rows[0].astype(jnp.float32).reshape(1, groups, head_size), cosine, sine_table
    ).astype(jnp.bfloat16)
    cache_len = cache_rows.shape[1]
    key_rows = jnp.concatenate(
        [cache_rows[0].reshape(cache_len, groups, head_size), rot_key], axis=0
    )
    value_rows = jnp.concatenate(
        [
            cache_rows[1].reshape(cache_len, groups, head_size),
            fresh_rows[1].reshape(1, groups, head_size),
        ],
        axis=0,
    )
    visible = jnp.concatenate(
        [jnp.arange(cache_len, dtype=jnp.int32)[None, :] < length, jnp.ones((1, 1), jnp.bool_)],
        axis=1,
    )
    return attend(rot_query, key_rows, value_rows, visible)[0]


def decode_attend(own_query, own_fresh, decode_cache, decode_length):

    def one_slot(query_rows, fresh_rows, cache_rows, length):
        return decode_task(query_rows, fresh_rows, cache_rows, length, HEAD_SIZE)

    return jax.vmap(one_slot)(own_query, own_fresh, decode_cache, decode_length)


def body(
    prefill_query,
    prefill_new_pairs,
    prefill_cache,
    prefill_start,
    decode_query,
    decode_fresh,
    decode_cache,
    decode_length,
    decode_slot,
    prefill_states,
    decode_states,
    output_proj,
    norm_gain,
    gate_weight,
    up_weight,
    down_weight,
):
    local_prefills = prefill_query.shape[0] // REQUEST_TOKENS
    query_blocks = prefill_query.reshape(local_prefills, REQUEST_TOKENS, prefill_query.shape[1])
    newest_blocks = prefill_new_pairs.reshape(
        local_prefills, REQUEST_TOKENS, 2, prefill_new_pairs.shape[2]
    )
    prefill_att = lax.map(
        lambda operands: prefill_task(
            operands[0], operands[1], operands[2], operands[3], HEAD_SIZE
        ),
        (query_blocks, newest_blocks, prefill_cache, prefill_start),
    )
    prefill_att = prefill_att.reshape(local_prefills * REQUEST_TOKENS, prefill_query.shape[1])
    local_decodes = decode_query.shape[0]
    fresh_width = decode_fresh.shape[2]
    fresh_flat = decode_fresh.reshape(local_decodes, 2 * fresh_width)
    slot_marks = decode_slot.astype(jnp.bfloat16)
    every_query, every_fresh, every_slot = (
        lax.all_gather(decode_query, "req", axis=0, tiled=True),
        lax.all_gather(fresh_flat, "req", axis=0, tiled=True),
        lax.all_gather(slot_marks, "req", axis=0, tiled=True),
    )
    owned = lax.axis_index("req") * local_decodes + jnp.arange(local_decodes, dtype=jnp.int32)
    picker = (every_slot.astype(jnp.int32)[None, :] == owned[:, None]).astype(jnp.bfloat16)
    own_query = jnp.dot(picker, every_query, preferred_element_type=jnp.float32).astype(
        jnp.bfloat16
    )
    own_fresh = jnp.dot(picker, every_fresh, preferred_element_type=jnp.float32).astype(
        jnp.bfloat16
    )
    own_att = decode_attend(
        own_query, own_fresh.reshape(local_decodes, 2, fresh_width), decode_cache, decode_length
    )
    every_att = lax.all_gather(own_att, "req", axis=0, tiled=True)
    total_slots = every_att.shape[0]
    chooser = (decode_slot[:, None] == jnp.arange(total_slots, dtype=jnp.int32)[None, :]).astype(
        jnp.bfloat16
    )
    decode_att = jnp.dot(chooser, every_att, preferred_element_type=jnp.float32).astype(
        jnp.bfloat16
    )
    attended = jnp.concatenate([prefill_att, decode_att], axis=0)
    states = jnp.concatenate([prefill_states, decode_states], axis=0)
    partial_value = jnp.dot(
        attended,
        lax.all_gather(output_proj, "req", axis=1, tiled=True),
        preferred_element_type=jnp.float32,
    )
    model_width = partial_value.shape[1]
    share_cols = model_width // lax.axis_size("head")
    share_start = lax.axis_index("head") * share_cols
    own_block = lax.dynamic_slice_in_dim(partial_value, share_start, share_cols, 1) + states.astype(
        jnp.float32
    )
    placed = lax.dynamic_update_slice_in_dim(partial_value, own_block, share_start, 1)
    summed_full = lax.psum(placed, "head")
    mean_square = jnp.mean(summed_full * summed_full, axis=1, keepdims=True)
    normed = (
        summed_full * lax.rsqrt(mean_square + norm_eps) * norm_gain.astype(jnp.float32)
    ).astype(jnp.bfloat16)
    summed = lax.dynamic_slice_in_dim(summed_full, share_start, share_cols, 1)

    def add_rows(weight_piece):
        return jnp.dot(normed, weight_piece, preferred_element_type=jnp.float32)

    gate_sum = add_rows(lax.all_gather(gate_weight, "req", axis=0, tiled=True))
    upper = add_rows(lax.all_gather(up_weight, "req", axis=0, tiled=True))
    hidden = (jax.nn.silu(gate_sum) * upper).astype(jnp.bfloat16)
    down_terms = jnp.dot(
        hidden,
        lax.all_gather(down_weight, "req", axis=1, tiled=True),
        preferred_element_type=jnp.float32,
    )
    result = (
        summed + lax.psum_scatter(down_terms, "head", scatter_dimension=1, tiled=True)
    ).astype(jnp.bfloat16)
    prefill_rows = prefill_att.shape[0]
    return (result[:prefill_rows], result[prefill_rows:])


def solution(mesh):
    in_specs = (
        P("req", "head"),
        P("req", None, "head"),
        P("req", None, None, "head"),
        P("req"),
        P("req", "head"),
        P("req", None, "head"),
        P("req", None, None, "head"),
        P("req"),
        P("req"),
        P("req", "head"),
        P("req", "head"),
        P("head", "req"),
        P(),
        P("req", "head"),
        P("req", "head"),
        P("head", "req"),
    )
    out_specs = (P("req", "head"), P("req", "head"))
    return jax.shard_map(body, mesh=mesh, in_specs=in_specs, out_specs=out_specs, check_vma=False)
```

profile of v0, /device:TPU:1, one launch (start us, length us, event | category | flops | bytes accessed | tf_op | source)
XLA Modules:
  0.0 560.0 jit_solution(2752393943931964175)
XLA Ops:
  11.5 64.1 %all-reduce.1 = bf16[96]{0:T(256)(128)(2,1)S(1)} all-reduce(bf16[96]{0:T(256)(128)(2,1)S(1)} %dynamic-update-slice), channel_id=1, replica_groups=mesh['req'=32,'head'=4] {'req'}, use_global_device_ids=true, to_apply=%add.1 | all-reduce | flops 96 | bytes 384
  75.6 25.6 %all-gather.1 = bf16[32,3,512]{2,1,0:T(4,128)(2,1)S(1)} all-gather(bf16[1,3,512]{2,1,0:T(4,128)(2,1)} %bitcast.118), channel_id=1, replica_groups=mesh['req'=32,'head'=4] {'req'}, dimensions={0}, use_global_device_ids=true | all-gather | bytes 101376 | tf_op jit(solution)/shard_map/all_gather | solution.py:156
  103.5 3.0 fusion.89
  108.5 3.1 fusion.88
  112.9 25.6 %all-gather = bf16[32,3,512]{2,1,0:T(4,128)(2,1)S(1)} all-gather(bf16[1,3,512]{2,1,0:T(4,128)(2,1)S(1)} %reshape.338), channel_id=1, replica_groups=mesh['req'=32,'head'=4] {'req'}, dimensions={0}, use_global_device_ids=true | all-gather | bytes 101376 | tf_op jit(solution)/shard_map/all_gather | solution.py:157
  140.9 5.8 %fusion.87 = (bf16[3,1,2048,256]{3,2,1,0:T(8,128)(2,1)}, bf16[3,1,2048,256]{3,2,1,0:T(8,128)(2,1)}) fusion(bf16[3,2,2048,256]{3,2,1,0:T(8,128)(2,1)} %param.22), kind=kLoop, calls=%fused_computation.112 | loop fusion | bytes 12582912 | tf_op jit(solution)/shard_map/vmap()/slice | solution.py:97
  146.7 3.2 copy.81
  149.9 2.8 copy.73
  152.7 3.2 copy.80
  155.9 2.8 copy.71
  158.9 3.1 fusion.90
  162.9 22.5 %all-gather.2 = bf16[32,3,512]{2,1,0:T(4,128)(2,1)S(1)} all-gather(bf16[1,3,512]{2,1,0:T(4,128)(2,1)S(1)} %reshape.342), channel_id=1, replica_groups=mesh['req'=32,'head'=4] {'req'}, dimensions={0}, use_global_device_ids=true | all-gather | bytes 101376 | tf_op jit(solution)/shard_map/all_gather | solution.py:171
  203.4 12.7 %fusion.2 = (f32[2,2,512]{2,1,0:T(2,128)S(1)}, f32[2,2560,512,2]{2,1,3,0:T(8,128)}) fusion(pred[512,2560]{0,1:T(8,128)(4,1)S(1)} %pad_add_fusion, f32[512,2,2,64]{3,0,2,1:T(8,128)} %copy.68, f32[512,2,2,64]{3,0,2,1:T(8,128)} %copy.67, f32[512,2,2,128]{3,2,1,0:T(2,128)S(1)} %reshape.332, f32[512,128]{1,0:T(8,128)S(1)} %get-tuple-element.47, ...), kind=kOutput, calls=%fused_computation.4 | convolution fusion | flops 1361836032 | bytes 26222592 | tf_op jit(solution)/shard_map/while/body/eval_jaxpr/qhgd,khd->hgqk/dot_general | solution.py:35
  216.1 9.6 %fusion = f32[2,2,512]{2,1,0:T(2,128)S(1)} fusion(f32[2,2560,512,2]{2,1,3,0:T(8,128)} %get-tuple-element.43, f32[2,2,512]{2,1,0:T(2,128)S(1)} %get-tuple-element.42, pred[512,2560]{0,1:T(8,128)(4,1)S(1)} %pad_add_fusion), kind=kLoop, calls=%fused_computation.2 | loop fusion | flops 20969472 | bytes 22298624 | tf_op jit(solution)/shard_map/while/body/eval_jaxpr/reduce_sum | solution.py:41
  225.8 10.6 %fusion.28 = bf16[512,2,2,128]{0,3,2,1:T(8,128)(2,1)S(1)} fusion(f32[2,2560,512,2]{2,1,3,0:T(8,128)} %get-tuple-element.43, f32[2,2,512]{2,1,0:T(2,128)S(1)} %get-tuple-element.42, pred[512,2560]{0,1:T(8,128)(4,1)S(1)} %pad_add_fusion, bf16[512,2,128]{0,2,1:T(8,128)(2,1)S(1)} %bitcast.114, bf16[2048,2,128]{0,2,1:T(8,128)(2,1)S(1)} %bitcast.112, ...), kind=kOutput, calls=%fused_computation.32 | convolution fusion | flops 1366294528 | bytes 24133632 | tf_op jit(solution)/shard_map/while/body/eval_jaxpr/hgqk,khd->qhgd/dot_general | solution.py:43
  236.5 5.3 fusion.47
  246.3 91.8 %all-reduce.4.cloned.1.call-done = f32[515,2048]{1,0:T(8,128)} async-done(((f32[515,2048]{1,0:T(8,128)}), f32[515,2048]{1,0:T(8,128)}) %all-reduce.4.cloned.1.call-update) | async-done | bytes 4218896 | tf_op jit(solution)/shard_map/psum | solution.py:193
  338.1 2.6 multiply_reduce_fusion
  340.7 48.8 %all-gather.10.cloned.1.call-done = bf16[2048,1536]{1,0:T(8,128)(2,1)} async-done(((bf16[64,1536]{1,0:T(8,128)(2,1)}), bf16[2048,1536]{1,0:T(8,128)(2,1)}) %all-gather.10.cloned.1.call-update) | async-done | bytes 6291472 | tf_op jit(solution)/shard_map/all_gather | solution.py:203
  389.5 7.0 %fusion.86 = f32[515,1536]{1,0:T(8,128)S(1)} fusion(bf16[2048,1536]{1,0:T(8,128)(2,1)} %all-gather.10.cloned.1.call-done, f32[515,2048]{1,0:T(8,128)} %all-reduce.4.cloned.1.call-done, f32[2048]{0:T(1024)S(1)} %convert_element_type.169, f32[515]{0:T(1024)S(1)} %add_rsqrt_fusion), kind=kOutput, calls=%fused_computation.111 | convolution fusion | flops 3243264000 | bytes 13684748 | tf_op jit(solution)/shard_map/dot_general | solution.py:201
  396.5 42.8 %all-gather.12.cloned.1.call-done = bf16[2048,1536]{1,0:T(8,128)(2,1)} async-done(((bf16[64,1536]{1,0:T(8,128)(2,1)}), bf16[2048,1536]{1,0:T(8,128)(2,1)}) %all-gather.12.cloned.1.call-update) | async-done | bytes 6291472 | tf_op jit(solution)/shard_map/all_gather | solution.py:204
  439.3 49.8 %all-gather.14.cloned.1.call-done = bf16[1536,2048]{0,1:T(8,128)(2,1)} async-done(((bf16[1536,64]{0,1:T(8,128)(2,1)}), bf16[1536,2048]{0,1:T(8,128)(2,1)}) %all-gather.14.cloned.1.call-update) | async-done | bytes 6291472 | tf_op jit(solution)/shard_map/all_gather | solution.py:208
  489.1 14.8 %fusion.46 = f32[515,2048]{1,0:T(8,128)} fusion(bf16[1536,2048]{0,1:T(8,128)(2,1)} %all-gather.14.cloned.1.call-done, bf16[2048,1536]{1,0:T(8,128)(2,1)} %all-gather.12.cloned.1.call-done, f32[515,1536]{1,0:T(8,128)S(1)} %fusion.86, f32[515,2048]{1,0:T(8,128)} %all-reduce.4.cloned.1.call-done, f32[2048]{0:T(1024)S(1)} %convert_element_type.169, ...), kind=kOutput, calls=%fused_computation.48 | convolution fusion | flops 6488110080 | bytes 24195084 | tf_op jit(solution)/shard_map/dot_general | solution.py:206
  503.9 46.1 %reduce-scatter.2.cloned.1.call-done = f32[515,512]{1,0:T(8,128)} async-done(((f32[515,2048]{1,0:T(8,128)}), f32[515,512]{1,0:T(8,128)}) %reduce-scatter.2.cloned.1.call-update) | async-done | bytes 1054736 | tf_op jit(solution)/shard_map/reduce_scatter | solution.py:212
  (103 shorter events, 37.6 us)
Async XLA Ops:
  7.2 229.3 %all-gather.8.cloned.1.call-start = ((), (), s32[]{:S(2)}) async-start(), calls=%async_computation.1 | async-start | bytes 2162688 | tf_op jit(solution)/shard_map/all_gather | solution.py:183
  7.9 330.2 %all-reduce.4.cloned.1.call-start = ((), (), s32[]{:S(2)}) async-start(), calls=%async_computation.2 | async-start | bytes 8519680 | tf_op jit(solution)/shard_map/psum | solution.py:193
  107.3 4.4 copy-start
  107.3 4.2 copy-start.3
  108.5 4.4 copy-start.15
  158.9 3.4 copy-start.2
  162.2 23.2 %copy-start.9 = (f32[512,64]{1,0:T(8,128)S(1)}, f32[512,64]{1,0:T(8,128)}, u32[]{:S(2)}) copy-start(f32[512,64]{1,0:T(8,128)} %get-tuple-element.36) | copy-start | bytes 393220
  162.2 23.2 %copy-start.10 = (f32[512,64]{1,0:T(8,128)S(1)}, f32[512,64]{1,0:T(8,128)}, u32[]{:S(2)}) copy-start(f32[512,64]{1,0:T(8,128)} %get-tuple-element.37) | copy-start | bytes 393220
  162.8 24.9 %copy-start.1 = (f32[512,2,128]{2,0,1:T(8,128)S(1)}, f32[512,2,128]{2,0,1:T(8,128)}, u32[]{:S(2)}) copy-start(f32[512,2,128]{2,0,1:T(8,128)} %copy-done) | copy-start | bytes 1572868
  162.8 24.9 %copy-start.5 = (f32[512,2,64]{2,0,1:T(8,128)S(1)}, f32[512,2,64]{2,0,1:T(8,128)}, u32[]{:S(2)}) copy-start(f32[512,2,64]{2,0,1:T(8,128)} %get-tuple-element.28) | copy-start | bytes 786436
  162.8 24.9 %copy-start.6 = (f32[512,2,64]{2,0,1:T(8,128)S(1)}, f32[512,2,64]{2,0,1:T(8,128)}, u32[]{:S(2)}) copy-start(f32[512,2,64]{2,0,1:T(8,128)} %get-tuple-element.29) | copy-start | bytes 786436
  162.9 25.8 %copy-start.16 = (s32[3]{0:T(128)S(1)}, s32[3]{0:T(128)}, u32[]{:S(2)}) copy-start(s32[3]{0:T(128)} %param.24) | copy-start | bytes 40
  190.5 7.1 %copy-start.4 = (f32[512,4,64]{0,2,1:T(8,128)S(1)}, f32[512,4,64]{0,2,1:T(8,128)}, u32[]{:S(2)}) copy-start(f32[512,4,64]{0,2,1:T(8,128)} %get-tuple-element.25) | copy-start | bytes 1572868
  199.0 4.4 copy-start.7
  216.1 9.6 %copy-start.8 = (bf16[1,1,2048,256]{2,3,1,0:T(8,128)(2,1)S(1)}, bf16[1,1,2048,256]{2,3,1,0:T(8,128)(2,1)}, u32[]{:S(2)}) copy-start(bf16[1,1,2048,256]{2,3,1,0:T(8,128)(2,1)} %copy.57) | copy-start | bytes 3145732
  216.1 9.6 %copy-start.12 = (bf16[512,1,256]{0,2,1:T(8,128)(2,1)S(1)}, bf16[512,1,256]{0,2,1:T(8,128)(2,1)}, u32[]{:S(2)}) copy-start(bf16[512,1,256]{0,2,1:T(8,128)(2,1)} %copy.58) | copy-start | bytes 786436
  236.4 5.3 copy-start.11
  236.5 5.3 copy-start.13
  241.8 4.5 copy-start.14
  244.3 145.2 %all-gather.10.cloned.1.call-start = ((), (), s32[]{:S(2)}) async-start(), calls=%async_computation.3 | async-start | bytes 6488064 | tf_op jit(solution)/shard_map/all_gather | solution.py:203
  245.0 194.3 %all-gather.12.cloned.1.call-start = ((), (), s32[]{:S(2)}) async-start(), calls=%async_computation.4 | async-start | bytes 6488064 | tf_op jit(solution)/shard_map/all_gather | solution.py:204
  245.6 243.5 %all-gather.14.cloned.1.call-start = ((), (), s32[]{:S(2)}) async-start(), calls=%async_computation.5 | async-start | bytes 6488064 | tf_op jit(solution)/shard_map/all_gather | solution.py:208
  246.2 303.9 %reduce-scatter.2.cloned.1.call-start = ((), (), s32[]{:S(2)}) async-start(), calls=%async_computation.6 | async-start | bytes 5324800 | tf_op jit(solution)/shard_map/reduce_scatter | solution.py:212
Sparse Core Ops, SparseCore 0:
  10.2 47.0 all-gather.7
  244.4 93.6 all-reduce.3
  340.4 49.0 all-gather.9
  391.6 47.6 all-gather.11
  441.4 47.6 all-gather.13
  504.0 45.9 reduce-scatter.1
where the time goes:
time: 561 us; the launch traced here: 560 us
  waiting for transfers between devices  282 us (50%)
  blocking collectives  138 us (25%)
  matrix products  54.7 us (10%)
  local copies, waits for them, and re-layouts  42.7 us (8%)
  other arithmetic  27.1 us (5%)
  between operations  15.7 us (3%)
    psum x1, waiting for transfers between devices, body(): summed_full = lax.psum(placed, 'head')  91.8 us
    unnamed x1, blocking collectives  64.1 us
    all_gather x1, waiting for transfers between devices, body(): lax.all_gather(down_weight, 'req', axis=1, tiled=True)  49.8 us
    all_gather x1, waiting for transfers between devices, body(): gate_sum = add_rows(lax.all_gather(gate_weight, 'req', axis=0, tiled=True))  48.8 us
    reduce_scatter x1, waiting for transfers between devices, body(): lax.psum_scatter(down_terms, 'head', scatter_dimension=1, tiled=True)  46.1 us
    all_gather x1, waiting for transfers between devices, body(): upper = add_rows(lax.all_gather(up_weight, 'req', axis=0, tiled=True))  42.8 us
    all_gather x1, blocking collectives, body(): lax.all_gather(fresh_flat, 'req', axis=0, tiled=True)  25.6 us
    all_gather x1, blocking collectives, body(): lax.all_gather(decode_query, 'req', axis=0, tiled=True)  25.6 us
  transfers between devices with their start and end apart: 6, of which 5 were waited for; matrix products, arithmetic and copies ran while one was open for 18% of the time, Pallas kernels for 0%

commit v1 on v0

--- a/solution.py
+++ b/solution.py
@@ -205,7 +205,9 @@
     hidden = (jax.nn.silu(gate_sum) * upper).astype(jnp.bfloat16)
     down_terms = jnp.dot(
         hidden,
-        lax.all_gather(down_weight, "req", axis=1, tiled=True),
+        jnp.concatenate(
+            lax.all_to_all(jnp.stack([down_weight] * lax.axis_size("req")), "req", 0, 0), axis=1
+        ),
         preferred_element_type=jnp.float32,
     )
     result = (

time: 561 us -> 511 us (0.911)
  waiting for transfers between devices: 282 us -> 224 us
    all_gather x1 -> x0, waiting for transfers between devices: 49.8 us -> none  [body(): lax.all_gather(down_weight, 'req', axis=1, tiled=True)]
    psum x1, waiting for transfers between devices: 91.8 us -> 84 us  [body(): summed_full = lax.psum(placed, 'head')]
    unnamed x46 -> x48, local copies, waits for them, and re-layouts: 11.3 us -> 11.3 us
  transfers between devices with their start and end apart: 6 -> 6, of which waited for: 5 -> 4; matrix products, arithmetic and copies ran while one was open for 18% -> 20% of each run, Pallas kernels for 0% -> 0%
where the time goes in v1:
time: 511 us; the launch traced here: 510 us
  waiting for transfers between devices  224 us (44%)
  blocking collectives  138 us (27%)
  matrix products  54.6 us (11%)
  local copies, waits for them, and re-layouts  46.3 us (9%)
  other arithmetic  27 us (5%)
  between operations  15.4 us (3%)
  starting transfers between devices  5.41 us (1%)
    psum x1, waiting for transfers between devices, body(): summed_full = lax.psum(placed, 'head')  84 us
    unnamed x1, blocking collectives  64.1 us
    all_gather x1, waiting for transfers between devices, body(): gate_sum = add_rows(lax.all_gather(gate_weight, 'req', axis=0, tiled=True))  48.8 us
    reduce_scatter x1, waiting for transfers between devices, body(): lax.psum_scatter(down_terms, 'head', scatter_dimension=1, tiled=True)  46.1 us
    all_gather x1, waiting for transfers between devices, body(): upper = add_rows(lax.all_gather(up_weight, 'req', axis=0, tiled=True))  42.8 us
    all_gather x1, blocking collectives, body(): lax.all_gather(fresh_flat, 'req', axis=0, tiled=True)  25.6 us
    all_gather x1, blocking collectives, body(): lax.all_gather(decode_query, 'req', axis=0, tiled=True)  25.6 us
    all_gather x1, blocking collectives, body(): every_att = lax.all_gather(own_att, 'req', axis=0, tiled=True)  22.5 us
  transfers between devices with their start and end apart: 6, of which 4 were waited for; matrix products, arithmetic and copies ran while one was open for 20% of the time, Pallas kernels for 0%

profile of v1, /device:TPU:1, one launch (start us, length us, event | category | flops | bytes accessed | tf_op | source)
XLA Modules:
  0.0 510.1 jit_solution(5682497568819913233)
XLA Ops:
  11.5 64.1 %all-reduce.1 = bf16[96]{0:T(256)(128)(2,1)S(1)} all-reduce(bf16[96]{0:T(256)(128)(2,1)S(1)} %dynamic-update-slice), channel_id=1, replica_groups=mesh['req'=32,'head'=4] {'req'}, use_global_device_ids=true, to_apply=%add.1 | all-reduce | flops 96 | bytes 384
  75.6 25.6 %all-gather.1 = bf16[32,3,512]{2,1,0:T(4,128)(2,1)S(1)} all-gather(bf16[1,3,512]{2,1,0:T(4,128)(2,1)} %bitcast.121), channel_id=1, replica_groups=mesh['req'=32,'head'=4] {'req'}, dimensions={0}, use_global_device_ids=true | all-gather | bytes 101376 | tf_op jit(solution)/shard_map/all_gather | solution.py:156
  103.5 3.1 fusion.89
  108.7 3.1 fusion.88
  113.1 25.6 %all-gather = bf16[32,3,512]{2,1,0:T(4,128)(2,1)S(1)} all-gather(bf16[1,3,512]{2,1,0:T(4,128)(2,1)S(1)} %reshape.348), channel_id=1, replica_groups=mesh['req'=32,'head'=4] {'req'}, dimensions={0}, use_global_device_ids=true | all-gather | bytes 101376 | tf_op jit(solution)/shard_map/all_gather | solution.py:157
  141.1 5.8 %fusion.87 = (bf16[3,1,2048,256]{3,2,1,0:T(8,128)(2,1)}, bf16[3,1,2048,256]{3,2,1,0:T(8,128)(2,1)}) fusion(bf16[3,2,2048,256]{3,2,1,0:T(8,128)(2,1)} %param.22), kind=kLoop, calls=%fused_computation.112 | loop fusion | bytes 12582912 | tf_op jit(solution)/shard_map/vmap()/slice | solution.py:97
  146.9 3.2 copy.82
  150.1 2.8 copy.74
  152.9 3.2 copy.81
  156.1 2.8 copy.72
  159.1 3.1 fusion.90
  163.1 22.5 %all-gather.2 = bf16[32,3,512]{2,1,0:T(4,128)(2,1)S(1)} all-gather(bf16[1,3,512]{2,1,0:T(4,128)(2,1)S(1)} %reshape.352), channel_id=1, replica_groups=mesh['req'=32,'head'=4] {'req'}, dimensions={0}, use_global_device_ids=true | all-gather | bytes 101376 | tf_op jit(solution)/shard_map/all_gather | solution.py:171
  203.6 12.7 %fusion.2 = (f32[2,2,512]{2,1,0:T(2,128)S(1)}, f32[2,2560,512,2]{2,1,3,0:T(8,128)}) fusion(pred[512,2560]{0,1:T(8,128)(4,1)S(1)} %pad_add_fusion, f32[512,2,2,64]{3,0,2,1:T(8,128)} %copy.69, f32[512,2,2,64]{3,0,2,1:T(8,128)} %copy.68, f32[512,2,2,128]{3,2,1,0:T(2,128)S(1)} %reshape.342, f32[512,128]{1,0:T(8,128)S(1)} %get-tuple-element.47, ...), kind=kOutput, calls=%fused_computation.4 | convolution fusion | flops 1361836032 | bytes 26222592 | tf_op jit(solution)/shard_map/while/body/eval_jaxpr/qhgd,khd->hgqk/dot_general | solution.py:35
  216.3 9.6 %fusion = f32[2,2,512]{2,1,0:T(2,128)S(1)} fusion(f32[2,2560,512,2]{2,1,3,0:T(8,128)} %get-tuple-element.43, f32[2,2,512]{2,1,0:T(2,128)S(1)} %get-tuple-element.42, pred[512,2560]{0,1:T(8,128)(4,1)S(1)} %pad_add_fusion), kind=kLoop, calls=%fused_computation.2 | loop fusion | flops 20969472 | bytes 22298624 | tf_op jit(solution)/shard_map/while/body/eval_jaxpr/reduce_sum | solution.py:41
  225.9 10.6 %fusion.28 = bf16[512,2,2,128]{0,3,2,1:T(8,128)(2,1)S(1)} fusion(f32[2,2560,512,2]{2,1,3,0:T(8,128)} %get-tuple-element.43, f32[2,2,512]{2,1,0:T(2,128)S(1)} %get-tuple-element.42, pred[512,2560]{0,1:T(8,128)(4,1)S(1)} %pad_add_fusion, bf16[512,2,128]{0,2,1:T(8,128)(2,1)S(1)} %bitcast.117, bf16[2048,2,128]{0,2,1:T(8,128)(2,1)S(1)} %bitcast.115, ...), kind=kOutput, calls=%fused_computation.32 | convolution fusion | flops 1366294528 | bytes 24133632 | tf_op jit(solution)/shard_map/while/body/eval_jaxpr/hgqk,khd->qhgd/dot_general | solution.py:43
  236.6 5.2 %fusion.47 = f32[515,2048]{1,0:T(8,128)} fusion(bf16[512,2048]{0,1:T(8,128)(2,1)} %all-gather.7.cloned.1.call-done, bf16[3,512]{0,1:T(8,128)(2,1)S(1)} %copy.75, bf16[512,512]{0,1:T(8,128)(2,1)S(1)} %bitcast.116), kind=kOutput, calls=%fused_computation.49 | convolution fusion | flops 1081088000 | bytes 6843392 | tf_op jit(solution)/shard_map/dot_general | solution.py:181
  245.7 3.3 stack.2
  249.0 5.2 %all-to-all-start = ((bf16[32,1536,64]{1,2,0:T(8,128)(2,1)}), bf16[32,1536,64]{1,2,0:T(8,128)(2,1)}, u32[]{:S(2)}, u32[]{:S(2)}) async-start(bf16[32,1536,64]{1,2,0:T(8,128)(2,1)} %stack.2), calls=%async_computation | async-start | bytes 12582912 | tf_op jit(solution)/shard_map/all_to_all | solution.py:209
  254.3 84.0 %all-reduce.4.cloned.1.call-done = f32[515,2048]{1,0:T(8,128)} async-done(((f32[515,2048]{1,0:T(8,128)}), f32[515,2048]{1,0:T(8,128)}) %all-reduce.4.cloned.1.call-update) | async-done | bytes 4218896 | tf_op jit(solution)/shard_map/psum | solution.py:193
  340.8 48.8 %all-gather.9.cloned.1.call-done = bf16[2048,1536]{1,0:T(8,128)(2,1)} async-done(((bf16[64,1536]{1,0:T(8,128)(2,1)}), bf16[2048,1536]{1,0:T(8,128)(2,1)}) %all-gather.9.cloned.1.call-update) | async-done | bytes 6291472 | tf_op jit(solution)/shard_map/all_gather | solution.py:203
  389.7 7.0 %fusion.86 = f32[515,1536]{1,0:T(8,128)S(1)} fusion(bf16[2048,1536]{1,0:T(8,128)(2,1)} %all-gather.9.cloned.1.call-done, f32[515,2048]{1,0:T(8,128)} %all-reduce.4.cloned.1.call-done, f32[2048]{0:T(1024)S(1)} %convert_element_type.169, f32[515]{0:T(1024)S(1)} %add_rsqrt_fusion), kind=kOutput, calls=%fused_computation.111 | convolution fusion | flops 3243264000 | bytes 13684748 | tf_op jit(solution)/shard_map/dot_general | solution.py:201
  396.7 42.8 %all-gather.11.cloned.1.call-done = bf16[2048,1536]{1,0:T(8,128)(2,1)} async-done(((bf16[64,1536]{1,0:T(8,128)(2,1)}), bf16[2048,1536]{1,0:T(8,128)(2,1)}) %all-gather.11.cloned.1.call-update) | async-done | bytes 6291472 | tf_op jit(solution)/shard_map/all_gather | solution.py:204
  439.5 14.8 %fusion.46 = f32[515,2048]{1,0:T(8,128)} fusion(bf16[1536,2048]{0,1:T(8,128)(2,1)} %bitcast.37, bf16[2048,1536]{1,0:T(8,128)(2,1)} %all-gather.11.cloned.1.call-done, f32[515,1536]{1,0:T(8,128)S(1)} %fusion.86, f32[515,2048]{1,0:T(8,128)} %all-reduce.4.cloned.1.call-done, f32[2048]{0:T(1024)S(1)} %convert_element_type.169, f32[515]{0:T(1024)S(1)} %add_rsqrt_fusion), kind=kOutput, calls=%fused_computation.48 | convolution fusion | flops 6488110080 | bytes 24195084 | tf_op jit(solution)/shard_map/dot_general | solution.py:206
  454.3 46.1 %reduce-scatter.2.cloned.1.call-done = f32[515,512]{1,0:T(8,128)} async-done(((f32[515,2048]{1,0:T(8,128)}), f32[515,512]{1,0:T(8,128)}) %reduce-scatter.2.cloned.1.call-update) | async-done | bytes 1054736 | tf_op jit(solution)/shard_map/reduce_scatter | solution.py:214
  (105 shorter events, 39.6 us)
Async XLA Ops:
  7.2 229.5 %all-gather.7.cloned.1.call-start = ((), (), s32[]{:S(2)}) async-start(), calls=%async_computation.2 | async-start | bytes 2162688 | tf_op jit(solution)/shard_map/all_gather | solution.py:183
  7.9 330.4 %all-reduce.4.cloned.1.call-start = ((), (), s32[]{:S(2)}) async-start(), calls=%async_computation.3 | async-start | bytes 8519680 | tf_op jit(solution)/shard_map/psum | solution.py:193
  107.5 4.4 copy-start
  107.5 4.2 copy-start.3
  108.7 4.4 copy-start.16
  159.1 3.4 copy-start.2
  162.4 23.2 %copy-start.9 = (f32[512,64]{1,0:T(8,128)S(1)}, f32[512,64]{1,0:T(8,128)}, u32[]{:S(2)}) copy-start(f32[512,64]{1,0:T(8,128)} %get-tuple-element.36) | copy-start | bytes 393220
  162.4 23.2 %copy-start.10 = (f32[512,64]{1,0:T(8,128)S(1)}, f32[512,64]{1,0:T(8,128)}, u32[]{:S(2)}) copy-start(f32[512,64]{1,0:T(8,128)} %get-tuple-element.37) | copy-start | bytes 393220
  163.0 24.9 %copy-start.1 = (f32[512,2,128]{2,0,1:T(8,128)S(1)}, f32[512,2,128]{2,0,1:T(8,128)}, u32[]{:S(2)}) copy-start(f32[512,2,128]{2,0,1:T(8,128)} %copy-done) | copy-start | bytes 1572868
  163.0 24.9 %copy-start.5 = (f32[512,2,64]{2,0,1:T(8,128)S(1)}, f32[512,2,64]{2,0,1:T(8,128)}, u32[]{:S(2)}) copy-start(f32[512,2,64]{2,0,1:T(8,128)} %get-tuple-element.28) | copy-start | bytes 786436
  163.0 24.9 %copy-start.6 = (f32[512,2,64]{2,0,1:T(8,128)S(1)}, f32[512,2,64]{2,0,1:T(8,128)}, u32[]{:S(2)}) copy-start(f32[512,2,64]{2,0,1:T(8,128)} %get-tuple-element.29) | copy-start | bytes 786436
  163.0 25.8 %copy-start.17 = (s32[3]{0:T(128)S(1)}, s32[3]{0:T(128)}, u32[]{:S(2)}) copy-start(s32[3]{0:T(128)} %param.24) | copy-start | bytes 40
  190.7 7.1 %copy-start.4 = (f32[512,4,64]{0,2,1:T(8,128)S(1)}, f32[512,4,64]{0,2,1:T(8,128)}, u32[]{:S(2)}) copy-start(f32[512,4,64]{0,2,1:T(8,128)} %get-tuple-element.25) | copy-start | bytes 1572868
  199.2 4.4 copy-start.7
  216.3 9.6 %copy-start.8 = (bf16[1,1,2048,256]{2,3,1,0:T(8,128)(2,1)S(1)}, bf16[1,1,2048,256]{2,3,1,0:T(8,128)(2,1)}, u32[]{:S(2)}) copy-start(bf16[1,1,2048,256]{2,3,1,0:T(8,128)(2,1)} %copy.58) | copy-start | bytes 3145732
  216.3 9.6 %copy-start.12 = (bf16[512,1,256]{0,2,1:T(8,128)(2,1)S(1)}, bf16[512,1,256]{0,2,1:T(8,128)(2,1)}, u32[]{:S(2)}) copy-start(bf16[512,1,256]{0,2,1:T(8,128)(2,1)} %copy.59) | copy-start | bytes 786436
  236.6 5.3 %copy-start.11 = (bf16[512,512]{1,0:T(8,128)(2,1)S(1)}, bf16[512,512]{1,0:T(8,128)(2,1)}, u32[]{:S(2)}) copy-start(bf16[512,512]{1,0:T(8,128)(2,1)} %param.25) | copy-start | bytes 1572868
  236.6 5.2 %copy-start.14 = (bf16[3,512]{1,0:T(4,128)(2,1)S(1)}, bf16[3,512]{1,0:T(4,128)(2,1)}, u32[]{:S(2)}) copy-start(bf16[3,512]{1,0:T(4,128)(2,1)} %param.26) | copy-start | bytes 9220
  241.9 3.8 copy-start.13
  244.3 145.3 %all-gather.9.cloned.1.call-start = ((), (), s32[]{:S(2)}) async-start(), calls=%async_computation.4 | async-start | bytes 6488064 | tf_op jit(solution)/shard_map/all_gather | solution.py:203
  245.1 194.4 %all-gather.11.cloned.1.call-start = ((), (), s32[]{:S(2)}) async-start(), calls=%async_computation.5 | async-start | bytes 6488064 | tf_op jit(solution)/shard_map/all_gather | solution.py:204
  249.0 5.3 %copy-start.15 = (bf16[2048]{0:T(1024)(128)(2,1)S(1)}, bf16[2048]{0:T(1024)(128)(2,1)}, u32[]{:S(2)}) copy-start(bf16[2048]{0:T(1024)(128)(2,1)} %param.28) | copy-start | bytes 12292
  249.0 147.7 %all-to-all-start = ((bf16[32,1536,64]{1,2,0:T(8,128)(2,1)}), bf16[32,1536,64]{1,2,0:T(8,128)(2,1)}, u32[]{:S(2)}, u32[]{:S(2)}) async-start(bf16[32,1536,64]{1,2,0:T(8,128)(2,1)} %stack.2), calls=%async_computation | async-start | bytes 12582912 | tf_op jit(solution)/shard_map/all_to_all | solution.py:209
  254.2 246.2 %reduce-scatter.2.cloned.1.call-start = ((), (), s32[]{:S(2)}) async-start(), calls=%async_computation.6 | async-start | bytes 5324800 | tf_op jit(solution)/shard_map/reduce_scatter | solution.py:214
Sparse Core Ops, SparseCore 0:
  10.2 47.0 all-gather.6
  244.5 93.7 all-reduce.3
  340.5 49.0 all-gather.8
  391.8 47.6 all-gather.10
  454.4 45.9 reduce-scatter.1
